TPU v7x, 32 devices: a whole 2x2x4 slice. The times are simulated.
32 devices in a mesh: req: 32 (over z, y, x, core).
Axes of the slice: x: 2, y: 2, z: 4, core: 2. Of those that a mesh axis runs over, the one named last changes fastest.
Arguments:
- hidden_in: bfloat16 [16384, 2048], P('req'), may hold values from -6 to 6
- qkv: bfloat16 [16384, 6144], P('req'), may hold values from -400 to 400
- cache: bfloat16 [128, 128, 4096], P('req'), may hold values from -400 to 400
- lengths: int32 [128], P('req'), may hold values from 2 to 128, as said below
- prefill_flag: int32 [32], P('req'), may hold values 0 or 1
- cache_slot: int32 [128], P('req'), may hold values from 0 to 127, as said below
- slot_owner: int32 [128], P('req'), may hold values from 0 to 127, as said below
- out_weight: bfloat16 [2048, 2048], replicated, may hold values from -0.125 to 0.125
Outputs:
- layer_out: bfloat16 [16384, 2048], P('req')
Inputs may be any that keep to these rules, and one draw needn't show every extreme that they name: Each slot stores exactly one request's cache; of each device's 4 requests, at least half have their cache in a slot of their own device, drawn which; slot_owner[cache_slot[r]] = r. `slot_owner`: the inverse of cache_slot. `lengths`: some slot holds exactly 128 valid positions.
All inputs are finite; a program needn't handle non-finite values. No bound on the sum of `prefill_flag` on one device may be relied on, other than what follows from the above.
Results may differ from a plain program's by a relative error of at most 0.0034.
Values may be sent and summed in bfloat16 or wider, within the bound.
A program may use at most 128 MiB of HBM per device.

v0:
```python
import math
import jax
import jax.numpy as jnp
from jax import lax
from jax.sharding import PartitionSpec as P

D = 2048
H = 16
HD = 128
TOK_DEV = 512
RD = 4
LMAX = 128


def prefill_attention(block):
    score_scale = 1.0 / math.sqrt(HD)
    queries = block[:, :D].reshape(TOK_DEV, H, HD)
    keys_new = block[:, D : 2 * D].reshape(TOK_DEV, H, HD)
    values_new = block[:, 2 * D :].reshape(TOK_DEV, H, HD)
    scores = (
        jnp.einsum("qhd,khd->hqk", queries, keys_new, preferred_element_type=jnp.float32)
        * score_scale
    )
    causal = jnp.arange(TOK_DEV)[:, None] >= jnp.arange(TOK_DEV)[None, :]
    scores = jnp.where(causal[None], scores, -jnp.inf)
    top_score = jnp.max(scores, axis=-1, keepdims=True)
    expon = jnp.exp(scores - top_score)
    totals = jnp.sum(expon, axis=-1)
    summed = jnp.einsum(
        "hqk,khd->qhd", expon.astype(jnp.bfloat16), values_new, preferred_element_type=jnp.float32
    )
    result = summed / jnp.transpose(totals)[:, :, None]
    return result.reshape(TOK_DEV, D).astype(jnp.bfloat16)


def holder_partial(queries, cache, lengths):
    score_scale = 1.0 / math.sqrt(HD)
    query_heads = queries.reshape(RD, H, HD)
    cache_keys = cache[:, :, :D].reshape(RD, LMAX, H, HD)
    cache_values = cache[:, :, D:].reshape(RD, LMAX, H, HD)
    scores = (
        jnp.einsum("rhd,rlhd->rhl", query_heads, cache_keys, preferred_element_type=jnp.float32)
        * score_scale
    )
    valid = jnp.arange(LMAX, dtype=jnp.int32)[None, None, :] < lengths[:, None, None]
    scores = jnp.where(valid, scores, -jnp.inf)
    cache_max = jnp.max(scores, axis=-1)
    expon = jnp.exp(scores - cache_max[..., None])
    cache_total = jnp.sum(expon, axis=-1)
    cache_out = jnp.einsum(
        "rhl,rlhd->rhd",
        expon.astype(jnp.bfloat16),
        cache_values,
        preferred_element_type=jnp.float32,
    )
    return (cache_out.reshape(RD, D), cache_max, cache_total)


def combine_own(request_rows, cache_out, cache_max, cache_total):
    score_scale = 1.0 / math.sqrt(HD)
    query_heads = request_rows[:, :D].reshape(RD, H, HD).astype(jnp.float32)
    keys_new = request_rows[:, D : 2 * D].reshape(RD, H, HD).astype(jnp.float32)
    values_new = request_rows[:, 2 * D :].reshape(RD, H, HD).astype(jnp.float32)
    own_score = jnp.sum(query_heads * keys_new, axis=-1) * score_scale
    joint_max = jnp.maximum(cache_max, own_score)
    cache_factor = jnp.exp(cache_max - joint_max)
    own_factor = jnp.exp(own_score - joint_max)
    numer = (
        cache_out.reshape(RD, H, HD) * cache_factor[..., None] + own_factor[..., None] * values_new
    )
    denom = cache_total * cache_factor + own_factor
    return (numer / denom[..., None]).reshape(RD, D).astype(jnp.bfloat16)


def local(hidden_in, qkv, cache, lengths, prefill_flag, cache_slot, slot_owner, out_weight):
    request_rows = qkv[:RD]
    every_query = lax.all_gather(request_rows[:, :D], "req", axis=0, tiled=True)
    held_queries = every_query[slot_owner]
    part_out, part_max, part_total = holder_partial(held_queries, cache, lengths)
    every_out, every_max, every_total = (
        lax.all_gather(part_out.astype(jnp.bfloat16), "req", axis=0, tiled=True).astype(
            part_out.dtype
        ),
        lax.all_gather(part_max.astype(jnp.bfloat16), "req", axis=0, tiled=True).astype(
            part_max.dtype
        ),
        lax.all_gather(part_total.astype(jnp.bfloat16), "req", axis=0, tiled=True).astype(
            part_total.dtype
        ),
    )
    decode_att = combine_own(
        request_rows, every_out[cache_slot], every_max[cache_slot], every_total[cache_slot]
    )
    is_prefill = prefill_flag[0] == 1

    def prefill_path(block):
        attended = prefill_attention(block)
        return jnp.dot(attended, out_weight, preferred_element_type=jnp.float32).astype(
            jnp.bfloat16
        )

    def decode_path(block):
        live = jnp.dot(decode_att, out_weight, preferred_element_type=jnp.float32).astype(
            jnp.bfloat16
        )
        return jnp.concatenate([live, jnp.zeros((TOK_DEV - RD, D), jnp.bfloat16)], axis=0)

    projected = lax.cond(is_prefill, prefill_path, decode_path, qkv)
    summed = hidden_in.astype(jnp.float32) + projected.astype(jnp.float32)
    return summed.astype(jnp.bfloat16)


def solution(mesh):
    placed = (
        P("req", None),
        P("req", None),
        P("req", None, None),
        P("req"),
        P("req"),
        P("req"),
        P("req"),
        P(),
    )
    return jax.shard_map(
        local, mesh=mesh, in_specs=placed, out_specs=P("req", None), check_vma=False
    )
```

profile of v0, /device:TPU:0, one launch (start us, length us, event | category | flops | bytes accessed | tf_op | source)
XLA Modules:
  0.0 231.2 jit_solution(15579366147625669525)
XLA Ops:
  0.7 0.7 iota_compare_fusion.1
  1.4 0.7 compare_select_fusion
  2.0 0.7 compare_select_fusion.1
  2.7 0.8 slice_bitcast_fusion.1
  3.5 0.8 multiply_bitcast_fusion
  4.3 0.1 bitcast_reduce_fusion
  4.4 44.6 %all-gather = bf16[32,4,2048]{2,1,0:T(4,128)(2,1)S(1)} all-gather(bf16[1,4,2048]{2,1,0:T(4,128)(2,1)S(1)} %slice_bitcast_fusion.1), channel_id=1, replica_groups=mesh['req'=32] {'req'}, dimensions={0}, use_global_device_ids=true | all-gather | bytes 540672 | tf_op jit(solution)/shard_map/all_gather | solution.py:77
  49.0 0.1 reshape.136
  49.1 0.6 gather_fusion
  49.7 4.9 %slice_bitcast_fusion = (bf16[4,16,16,8,128]{4,3,2,1,0:T(8,128)(2,1)}, bf16[4,128,2048]{2,1,0:T(8,128)(2,1)}) fusion(bf16[4,128,4096]{2,1,0:T(8,128)(2,1)} %param.12), kind=kLoop, calls=%fused_computation.27 | loop fusion | bytes 8388608
  54.6 3.0 %copy.32 = bf16[4,128,2048]{1,2,0:T(8,128)(2,1)S(1)} copy(bf16[4,128,2048]{2,1,0:T(8,128)(2,1)} %get-tuple-element.38) | data formatting | bytes 4194304 | tf_op jit(solution)/shard_map/reshape | solution.py:39
  57.6 0.6 fusion.30
  58.2 0.1 fusion.21
  58.3 0.2 fusion.24
  58.5 2.2 fusion.15
  60.8 36.7 %all-gather.3 = bf16[32,4,16]{2,1,0:T(4,128)(2,1)S(1)} all-gather(bf16[1,4,16]{2,1,0:T(4,128)(2,1)S(1)} %bitcast.80), channel_id=1, replica_groups=mesh['req'=32] {'req'}, dimensions={0}, use_global_device_ids=true | all-gather | bytes 4224 | tf_op jit(solution)/shard_map/all_gather | solution.py:87
  97.5 38.0 %all-gather.2 = bf16[32,4,16]{2,1,0:T(4,128)(2,1)S(1)} all-gather(bf16[1,4,16]{2,1,0:T(4,128)(2,1)S(1)} %convert_bitcast_fusion.1), channel_id=1, replica_groups=mesh['req'=32] {'req'}, dimensions={0}, use_global_device_ids=true | all-gather | bytes 4224 | tf_op jit(solution)/shard_map/all_gather | solution.py:84
  135.5 0.6 gather_fusion.2
  136.0 0.6 gather_fusion.3
  136.7 0.1 broadcast_bitcast_fusion
  136.8 38.1 %all-gather.1 = bf16[32,4,2048]{2,1,0:T(4,128)(2,1)S(1)} all-gather(bf16[1,4,2048]{2,1,0:T(4,128)(2,1)S(1)} %reshape.137), channel_id=1, replica_groups=mesh['req'=32] {'req'}, dimensions={0}, use_global_device_ids=true | all-gather | bytes 540672 | tf_op jit(solution)/shard_map/all_gather | solution.py:81
  174.9 0.6 gather_fusion.1
  175.5 0.8 fusion.20
  176.3 50.8 %conditional.1 = (f32[512,2048]{1,0:T(8,128)}) conditional(s32[]{:T(128)} %bitcast.6, (bf16[4,2048]{1,0:T(4,128)(2,1)S(1)}, bf16[2048,2048]{1,0:T(8,128)(2,1)}) %tuple.13, (bf16[512,6144]{1,0:T(8,128)(2,1)}, bf16[2048,2048]{1,0:T(8,128)(2,1)}) %tuple.14), branch_computations={%region_3.4_spmd, %region_4.7_spmd} | conditional | flops 6493028352 | bytes 99778568 | solution.py:108
  176.5 0.1 iota_compare_fusion
  176.6 8.8 %copy.22 = bf16[512,6144]{0,1:T(8,128)(2,1)} copy(bf16[512,6144]{1,0:T(8,128)(2,1)} %get-tuple-element.27) | data formatting | bytes 12582912 | tf_op jit(solution)/shard_map
  185.4 4.6 %fusion.29 = (bf16[512,2048]{0,1:T(8,128)(2,1)S(1)}, bf16[512,2048]{0,1:T(8,128)(2,1)S(1)}, bf16[512,2048]{0,1:T(8,128)(2,1)}) fusion(bf16[512,6144]{0,1:T(8,128)(2,1)} %copy.22), kind=kLoop, calls=%fused_computation.58 | loop fusion | bytes 12582912 | tf_op jit(solution)/shard_map/cond/branch_1_fun/slice | solution.py:18
  190.0 7.5 %fusion = (f32[16,512]{1,0:T(8,128)S(1)}, f32[16,512,512]{1,2,0:T(8,128)}) fusion(pred[512,512]{0,1:T(8,128)(4,1)S(1)} %iota_compare_fusion, bf16[512,16,128]{0,2,1:T(8,128)(2,1)S(1)} %bitcast.72, bf16[512,16,128]{0,2,1:T(8,128)(2,1)S(1)} %bitcast.71), kind=kOutput, calls=%fused_computation.8 | convolution fusion | flops 1086316544 | bytes 21266432 | tf_op jit(solution)/shard_map/cond/branch_1_fun/qhd,khd->hqk/dot_general | solution.py:21
  197.5 9.1 %fusion.1 = f32[16,512]{1,0:T(8,128)S(1)} fusion(f32[16,512,512]{1,2,0:T(8,128)} %get-tuple-element.36, f32[16,512]{1,0:T(8,128)S(1)} %get-tuple-element.35, pred[512,512]{0,1:T(8,128)(4,1)S(1)} %iota_compare_fusion), kind=kLoop, calls=%fused_computation.9 | loop fusion | flops 16769024 | bytes 17104896 | tf_op jit(solution)/shard_map/cond/branch_1_fun/reduce_sum | solution.py:28
  206.7 10.9 %fusion.9 = bf16[512,16,128]{0,2,1:T(8,128)(2,1)S(1)} fusion(bf16[512,16,128]{0,2,1:T(8,128)(2,1)} %bitcast.73, f32[16,512,512]{1,2,0:T(8,128)} %get-tuple-element.36, f32[16,512]{1,0:T(8,128)S(1)} %get-tuple-element.35, pred[512,512]{0,1:T(8,128)(4,1)S(1)} %iota_compare_fusion, f32[512,16]{0,1:T(8,128)S(1)} %bitcast.78), kind=kOutput, calls=%fused_computation.17 | convolution fusion | flops 1092616192 | bytes 21299200 | tf_op jit(solution)/shard_map/cond/branch_1_fun/hqk,khd->qhd/dot_general | solution.py:29
  217.6 9.4 %fusion.10 = f32[512,2048]{1,0:T(8,128)} fusion(bf16[512,2048]{0,1:T(8,128)(2,1)S(1)} %bitcast.81, bf16[2048,2048]{1,0:T(8,128)(2,1)} %get-tuple-element.20), kind=kOutput, calls=%fused_computation.19 | convolution fusion | flops 4297064448 | bytes 14680064 | tf_op jit(solution)/shard_map/cond/branch_1_fun/dot_general | solution.py:98
  227.1 4.2 %add_convert_fusion = bf16[512,2048]{1,0:T(8,128)(2,1)} fusion(f32[512,2048]{1,0:T(8,128)} %get-tuple-element.43, bf16[512,2048]{1,0:T(8,128)(2,1)S(1)} %copy-done), kind=kLoop, calls=%fused_computation.23 | loop fusion | flops 3145728 | bytes 8388608 | tf_op jit(solution)/shard_map/convert_element_type | solution.py:110
  (13 shorter events, 0.2 us)
Async XLA Ops:
  176.3 50.8 %copy-start = (bf16[512,2048]{1,0:T(8,128)(2,1)S(1)}, bf16[512,2048]{1,0:T(8,128)(2,1)}, u32[]{:S(2)}) copy-start(bf16[512,2048]{1,0:T(8,128)(2,1)} %param.10) | copy-start | bytes 6291460
where the time goes:
time: 232 us; the launch traced here: 231 us
  blocking collectives  157 us (68%)
  matrix products  30.8 us (13%)
  local copies, waits for them, and re-layouts  24.7 us (11%)
  other arithmetic  17.4 us (7%)
    all_gather x1, blocking collectives, local(): every_query = lax.all_gather(request_rows[:, :D], 'req', axis=0, tiled=True)  44.6 us
    all_gather x1, blocking collectives, local(): lax.all_gather(part_out.astype(jnp.bfloat16), 'req', axis=0, tiled=True)  38.1 us
    all_gather x1, blocking collectives, local(): lax.all_gather(part_max.astype(jnp.bfloat16), 'req', axis=0, tiled=True)  38 us
    all_gather x1, blocking collectives, local(): lax.all_gather(part_total.astype(jnp.bfloat16), 'req', axis=0, tiled=True)  36.7 us
    dot_general x1, matrix products, prefill_attention(): jnp.einsum('hqk,khd->qhd', expon.astype(jnp.bfloat16), values_new, prefer...  10.9 us
    dot_general x1, matrix products, prefill_path(): jnp.dot(attended, out_weight, preferred_element_type=jnp.float32)  9.44 us
    reduce_sum x1, other arithmetic, prefill_attention(): totals = jnp.sum(expon, axis=-1)  9.15 us
    another operation x1, local copies, waits for them, and re-layouts  8.85 us

commit v1 on v0

--- a/solution.py
+++ b/solution.py
@@ -1,3 +1,4 @@
+import functools
 import math
 import jax
 import jax.numpy as jnp
@@ -10,6 +11,24 @@
 TOK_DEV = 512
 RD = 4
 LMAX = 128
+
+
+def check_local_data(vals, dim_i):
+    w2 = lax.axis_size("req")
+    frame_out, z_new, r2 = (w2, lax.axis_index("req"), vals.shape[dim_i])
+    opened, taken_in = (vals, 1)
+    while taken_in < frame_out:
+        k_now = lax.ppermute(
+            opened,
+            axis_name="req",
+            perm=[(w, (w - taken_in) % frame_out) for w in range(frame_out)],
+        )
+        opened = jnp.concatenate([opened, k_now], axis=dim_i)
+        taken_in = 2 * taken_in
+    return jnp.roll(opened, z_new * r2, axis=dim_i)
+
+
+direct_wires = functools.partial(check_local_data, dim_i=0)
 
 
 def prefill_attention(block):
@@ -78,9 +97,7 @@
     held_queries = every_query[slot_owner]
     part_out, part_max, part_total = holder_partial(held_queries, cache, lengths)
     every_out, every_max, every_total = (
-        lax.all_gather(part_out.astype(jnp.bfloat16), "req", axis=0, tiled=True).astype(
-            part_out.dtype
-        ),
+        direct_wires(part_out.astype(jnp.bfloat16)).astype(part_out.dtype),
         lax.all_gather(part_max.astype(jnp.bfloat16), "req", axis=0, tiled=True).astype(
             part_max.dtype
         ),

time: 232 us -> 220 us (0.948)
  blocking collectives: 157 us -> 123 us
  waiting for transfers between devices: 0 us -> 22 us
    all_gather x1 -> x0, blocking collectives: 38.1 us -> none  [local(): lax.all_gather(part_out.astype(jnp.bfloat16), 'req', axis=0, tiled=True)]
    ppermute x0 -> x5, waiting for transfers between devices: none -> 22 us  [check_local_data(): lax.ppermute(opened, axis_name='req', perm=[(w, (w - taken_in) % frame_ou...]
    all_gather x1, blocking collectives: 38 us -> 41.7 us  [local(): lax.all_gather(part_max.astype(jnp.bfloat16), 'req', axis=0, tiled=True)]
    unnamed x8 -> x10, local copies, waits for them, and re-layouts: 5.91 us -> 5.89 us
  transfers between devices with their start and end apart: 0 -> 5, of which waited for: 0 -> 4; matrix products, arithmetic and copies ran while one was open for 0% -> 1% of each run, Pallas kernels for 0% -> 0%
where the time goes in v1:
time: 220 us; the launch traced here: 219 us
  blocking collectives  123 us (56%)
  matrix products  30.8 us (14%)
  local copies, waits for them, and re-layouts  25 us (11%)
  waiting for transfers between devices  22 us (10%)
  other arithmetic  17 us (8%)
    all_gather x1, blocking collectives, local(): every_query = lax.all_gather(request_rows[:, :D], 'req', axis=0, tiled=True)  44.6 us
    all_gather x1, blocking collectives, local(): lax.all_gather(part_max.astype(jnp.bfloat16), 'req', axis=0, tiled=True)  41.7 us
    all_gather x1, blocking collectives, local(): lax.all_gather(part_total.astype(jnp.bfloat16), 'req', axis=0, tiled=True)  36.6 us
    ppermute x5, waiting for transfers between devices, check_local_data(): lax.ppermute(opened, axis_name='req', perm=[(w, (w - taken_in) % frame_ou...  22 us
    dot_general x1, matrix products, prefill_attention(): jnp.einsum('hqk,khd->qhd', expon.astype(jnp.bfloat16), values_new, prefer...  10.9 us
    dot_general x1, matrix products, prefill_path(): jnp.dot(attended, out_weight, preferred_element_type=jnp.float32)  9.45 us
    reduce_sum x1, other arithmetic, prefill_attention(): totals = jnp.sum(expon, axis=-1)  9.15 us
    another operation x1, local copies, waits for them, and re-layouts  8.83 us
  transfers between devices with their start and end apart: 5, of which 4 were waited for; matrix products, arithmetic and copies ran while one was open for 1% of the time, Pallas kernels for 0%

profile of v1, /device:TPU:0, one launch (start us, length us, event | category | flops | bytes accessed | tf_op | source)
XLA Modules:
  0.0 219.1 jit_solution(1134519120935969911)
XLA Ops:
  0.0 0.7 iota_compare_fusion.1
  0.7 0.7 compare_select_fusion.1
  1.4 0.8 slice_bitcast_fusion.1
  2.2 44.6 %all-gather = bf16[32,4,2048]{2,1,0:T(4,128)(2,1)S(1)} all-gather(bf16[1,4,2048]{2,1,0:T(4,128)(2,1)S(1)} %slice_bitcast_fusion.1), channel_id=1, replica_groups=mesh['req'=32] {'req'}, dimensions={0}, use_global_device_ids=true | all-gather | bytes 540672 | tf_op jit(solution)/shard_map/all_gather | solution.py:96
  46.8 0.1 reshape.136
  46.9 0.6 gather_fusion
  47.5 4.8 %slice_bitcast_fusion = (bf16[4,16,16,8,128]{4,3,2,1,0:T(8,128)(2,1)}, bf16[4,128,2048]{2,1,0:T(8,128)(2,1)}) fusion(bf16[4,128,4096]{2,1,0:T(8,128)(2,1)} %param.12), kind=kLoop, calls=%fused_computation.27 | loop fusion | bytes 8388608
  52.4 3.0 %copy.32 = bf16[4,128,2048]{1,2,0:T(8,128)(2,1)S(1)} copy(bf16[4,128,2048]{2,1,0:T(8,128)(2,1)} %get-tuple-element.38) | data formatting | bytes 4194304 | tf_op jit(solution)/shard_map/reshape | solution.py:58
  55.4 0.6 fusion.30
  56.1 0.2 fusion.24
  56.3 2.2 %fusion.15 = f32[4,16,1,128]{3,2,1,0:T(1,128)S(1)} fusion(bf16[4,16,16,8,128]{4,3,2,1,0:T(8,128)(2,1)} %get-tuple-element.37, bf16[4,16,128,1]{2,1,0,3:T(8,128)(2,1)S(1)} %get-tuple-element.39), kind=kOutput, calls=%fused_computation.24 | convolution fusion | flops 2097152 | bytes 2146304 | tf_op jit(solution)/shard_map/rhl,rlhd->rhd/dot_general | solution.py:69
  58.7 0.8 multiply_bitcast_fusion
  59.5 0.6 collective-permute-done
  60.2 41.7 %all-gather.1 = bf16[32,4,16]{2,1,0:T(4,128)(2,1)S(1)} all-gather(bf16[1,4,16]{2,1,0:T(4,128)(2,1)S(1)} %convert_bitcast_fusion.2), channel_id=1, replica_groups=mesh['req'=32] {'req'}, dimensions={0}, use_global_device_ids=true | all-gather | bytes 4224 | tf_op jit(solution)/shard_map/all_gather | solution.py:101
  101.9 36.6 %all-gather.2 = bf16[32,4,16]{2,1,0:T(4,128)(2,1)S(1)} all-gather(bf16[1,4,16]{2,1,0:T(4,128)(2,1)S(1)} %bitcast.92), channel_id=1, replica_groups=mesh['req'=32] {'req'}, dimensions={0}, use_global_device_ids=true | all-gather | bytes 4224 | tf_op jit(solution)/shard_map/all_gather | solution.py:104
  138.6 0.6 gather_fusion.2
  139.1 0.6 gather_fusion.3
  139.9 4.2 %collective-permute-done.2 = bf16[16,2048]{1,0:T(8,128)(2,1)S(1)} collective-permute-done((bf16[16,2048]{1,0:T(8,128)(2,1)S(1)}, bf16[16,2048]{1,0:T(8,128)(2,1)S(1)}, u32[]{:S(2)}, u32[]{:S(2)}) %collective-permute-start.2) | collective-permute-done | bytes 65568 | tf_op jit(solution)/shard_map/ppermute | solution.py:21
  144.2 4.9 %collective-permute-done.3 = bf16[32,2048]{1,0:T(8,128)(2,1)S(1)} collective-permute-done((bf16[32,2048]{1,0:T(8,128)(2,1)S(1)}, bf16[32,2048]{1,0:T(8,128)(2,1)S(1)}, u32[]{:S(2)}, u32[]{:S(2)}) %collective-permute-start.3) | collective-permute-done | bytes 131104 | tf_op jit(solution)/shard_map/ppermute | solution.py:21
  150.1 12.2 %collective-permute-done.4 = bf16[64,2048]{1,0:T(8,128)(2,1)S(1)} collective-permute-done((bf16[64,2048]{1,0:T(8,128)(2,1)S(1)}, bf16[64,2048]{1,0:T(8,128)(2,1)S(1)}, u32[]{:S(2)}, u32[]{:S(2)}) %collective-permute-start.4) | collective-permute-done | bytes 262176 | tf_op jit(solution)/shard_map/ppermute | solution.py:21
  162.3 0.3 concatenate.29
  162.6 0.1 dynamic-slice_convert_fusion
  162.7 0.6 gather_fusion.1
  163.3 0.8 fusion.20
  164.1 50.8 %conditional.1 = (f32[512,2048]{1,0:T(8,128)}) conditional(s32[]{:T(128)} %bitcast.6, (bf16[4,2048]{1,0:T(4,128)(2,1)S(1)}, bf16[2048,2048]{1,0:T(8,128)(2,1)}) %tuple.13, (bf16[512,6144]{1,0:T(8,128)(2,1)}, bf16[2048,2048]{1,0:T(8,128)(2,1)}) %tuple.14), branch_computations={%region_3.4_spmd, %region_4.7_spmd} | conditional | flops 6493028352 | bytes 99778568 | solution.py:125
  164.4 8.8 %copy.22 = bf16[512,6144]{0,1:T(8,128)(2,1)} copy(bf16[512,6144]{1,0:T(8,128)(2,1)} %get-tuple-element.27) | data formatting | bytes 12582912 | tf_op jit(solution)/shard_map
  173.2 4.6 %fusion.29 = (bf16[512,2048]{0,1:T(8,128)(2,1)S(1)}, bf16[512,2048]{0,1:T(8,128)(2,1)S(1)}, bf16[512,2048]{0,1:T(8,128)(2,1)}) fusion(bf16[512,6144]{0,1:T(8,128)(2,1)} %copy.22), kind=kLoop, calls=%fused_computation.64 | loop fusion | bytes 12582912 | tf_op jit(solution)/shard_map/cond/branch_1_fun/slice | solution.py:37
  177.8 7.5 %fusion = (f32[16,512]{1,0:T(8,128)S(1)}, f32[16,512,512]{1,2,0:T(8,128)}) fusion(pred[512,512]{0,1:T(8,128)(4,1)S(1)} %iota_compare_fusion, bf16[512,16,128]{0,2,1:T(8,128)(2,1)S(1)} %bitcast.77, bf16[512,16,128]{0,2,1:T(8,128)(2,1)S(1)} %bitcast.76), kind=kOutput, calls=%fused_computation.8 | convolution fusion | flops 1086316544 | bytes 21266432 | tf_op jit(solution)/shard_map/cond/branch_1_fun/qhd,khd->hqk/dot_general | solution.py:40
  185.4 9.1 %fusion.1 = f32[16,512]{1,0:T(8,128)S(1)} fusion(f32[16,512,512]{1,2,0:T(8,128)} %get-tuple-element.36, f32[16,512]{1,0:T(8,128)S(1)} %get-tuple-element.35, pred[512,512]{0,1:T(8,128)(4,1)S(1)} %iota_compare_fusion), kind=kLoop, calls=%fused_computation.9 | loop fusion | flops 16769024 | bytes 17104896 | tf_op jit(solution)/shard_map/cond/branch_1_fun/reduce_sum | solution.py:47
  194.5 10.9 %fusion.9 = bf16[512,16,128]{0,2,1:T(8,128)(2,1)S(1)} fusion(bf16[512,16,128]{0,2,1:T(8,128)(2,1)} %bitcast.78, f32[16,512,512]{1,2,0:T(8,128)} %get-tuple-element.36, f32[16,512]{1,0:T(8,128)S(1)} %get-tuple-element.35, pred[512,512]{0,1:T(8,128)(4,1)S(1)} %iota_compare_fusion, f32[512,16]{0,1:T(8,128)S(1)} %bitcast.90), kind=kOutput, calls=%fused_computation.17 | convolution fusion | flops 1092616192 | bytes 21299200 | tf_op jit(solution)/shard_map/cond/branch_1_fun/hqk,khd->qhd/dot_general | solution.py:48
  205.4 9.4 %fusion.10 = f32[512,2048]{1,0:T(8,128)} fusion(bf16[512,2048]{0,1:T(8,128)(2,1)S(1)} %bitcast.93, bf16[2048,2048]{1,0:T(8,128)(2,1)} %get-tuple-element.20), kind=kOutput, calls=%fused_computation.19 | convolution fusion | flops 4297064448 | bytes 14680064 | tf_op jit(solution)/shard_map/cond/branch_1_fun/dot_general | solution.py:115
  214.9 4.2 %add_convert_fusion = bf16[512,2048]{1,0:T(8,128)(2,1)} fusion(f32[512,2048]{1,0:T(8,128)} %get-tuple-element.43, bf16[512,2048]{1,0:T(8,128)(2,1)S(1)} %copy-done), kind=kLoop, calls=%fused_computation.23 | loop fusion | flops 3145728 | bytes 8388608 | tf_op jit(solution)/shard_map/convert_element_type | solution.py:127
  (29 shorter events, 0.9 us)
Async XLA Ops:
  52.4 7.1 %copy-start.1 = (s32[4]{0:T(128)S(1)}, s32[4]{0:T(128)}, u32[]{:S(2)}) copy-start(s32[4]{0:T(128)} %param.15) | copy-start | bytes 52
  58.6 1.5 collective-permute-start
  60.1 79.6 %collective-permute-start.1 = (bf16[8,2048]{1,0:T(8,128)(2,1)S(1)}, bf16[8,2048]{1,0:T(8,128)(2,1)S(1)}, u32[]{:S(2)}, u32[]{:S(2)}) collective-permute-start(bf16[8,2048]{1,0:T(8,128)(2,1)S(1)} %pad_maximum_fusion.2), channel_id=1, source_target_pairs={{0,30},{1,31},{2,0},{3,1},{4,2},{5,3},{6,4},{7,5},{8,6},{9,7},{10,... | collective-permute-start | bytes 98312 | tf_op jit(solution)/shard_map/ppermute | solution.py:21
  139.7 4.4 %collective-permute-start.2 = (bf16[16,2048]{1,0:T(8,128)(2,1)S(1)}, bf16[16,2048]{1,0:T(8,128)(2,1)S(1)}, u32[]{:S(2)}, u32[]{:S(2)}) collective-permute-start(bf16[16,2048]{1,0:T(8,128)(2,1)S(1)} %pad_maximum_fusion.1), channel_id=1, source_target_pairs={{0,28},{1,29},{2,30},{3,31},{4,0},{5,1},{6,2},{7,3},{8,4},{9,5},{1... | collective-permute-start | bytes 196616 | tf_op jit(solution)/shard_map/ppermute | solution.py:21
  144.1 5.0 %collective-permute-start.3 = (bf16[32,2048]{1,0:T(8,128)(2,1)S(1)}, bf16[32,2048]{1,0:T(8,128)(2,1)S(1)}, u32[]{:S(2)}, u32[]{:S(2)}) collective-permute-start(bf16[32,2048]{1,0:T(8,128)(2,1)S(1)} %pad_maximum_fusion), channel_id=1, source_target_pairs={{0,24},{1,25},{2,26},{3,27},{4,28},{5,29},{6,30},{7,31},{8,0},{9,1... | collective-permute-start | bytes 393224 | tf_op jit(solution)/shard_map/ppermute | solution.py:21
  149.2 13.1 %collective-permute-start.4 = (bf16[64,2048]{1,0:T(8,128)(2,1)S(1)}, bf16[64,2048]{1,0:T(8,128)(2,1)S(1)}, u32[]{:S(2)}, u32[]{:S(2)}) collective-permute-start(bf16[64,2048]{1,0:T(8,128)(2,1)S(1)} %concatenate.28), channel_id=1, source_target_pairs={{0,16},{1,17},{2,18},{3,19},{4,20},{5,21},{6,22},{7,23},{8,24},{9,... | collective-permute-start | bytes 786440 | tf_op jit(solution)/shard_map/ppermute | solution.py:21
  164.1 50.8 %copy-start = (bf16[512,2048]{1,0:T(8,128)(2,1)S(1)}, bf16[512,2048]{1,0:T(8,128)(2,1)}, u32[]{:S(2)}) copy-start(bf16[512,2048]{1,0:T(8,128)(2,1)} %param.10) | copy-start | bytes 6291460
